TPU v7x, 32 devices: a whole 2x2x4 slice. The times are simulated.
32 devices in a mesh: groups: 2 (over x), tgt: 16 (over z, y, core).
Axes of the slice: x: 2, y: 2, z: 4, core: 2. Of those that a mesh axis runs over, the one named last changes fastest.
Arguments:
- source_feats: bfloat16 [4096, 1024], P(('groups', 'tgt')), parts along dimension 0, may hold values from -18 to 18
- target_feats: bfloat16 [16384, 1024], P(('groups', 'tgt')), parts along dimension 0, may hold values from -18 to 18
- source_logits: float32 [4096], P('groups'), parts along dimension 0, may hold values from -1.2 to 1.2
- target_logits: float32 [16384], P(('groups', 'tgt')), parts along dimension 0, may hold values from -1 to 3.4
Outputs:
- grad_source: float32 [4096, 1024], P(('groups', 'tgt')), parts along dimension 0
- grad_target: float32 [16384, 1024], P(('groups', 'tgt')), parts along dimension 0
- potential_src: float32 [4096], P('groups'), parts along dimension 0
- potential_tgt: float32 [16384], P(('groups', 'tgt')), parts along dimension 0
There are 2 independent parts, one for each index of `groups`. A program takes and returns all parts, laid end to end along the dimension named above; each array names one. Nothing has to cross between parts.
All inputs are finite; a program needn't handle non-finite values.
Results may differ from a plain program's by a relative error of at most 0.0033.
Values may be sent and summed in bfloat16 or wider, within the bound.
No kernel may reach another device: no remote copies, remote signals or barrier semaphores. Data moves between devices by JAX's collectives and lax.ppermute only.
A program may use at most 64 MiB of HBM per device.

v0:
```python
import math
import jax
import jax.numpy as jnp
from jax import lax
from jax.sharding import PartitionSpec as P

ITERS = 3


def per_device(source_feats, target_feats, source_logits, target_logits):
    width = target_feats.shape[1]
    scale = 1.0 / math.sqrt(width)
    source_count = source_feats.shape[0] * lax.axis_size("tgt")
    target_count = target_feats.shape[0] * lax.axis_size("tgt")
    log_source = source_logits - jnp.log(jnp.sum(jnp.exp(source_logits)))
    target_total = lax.psum(jnp.sum(jnp.exp(target_logits)), "tgt")
    log_target = target_logits - jnp.log(target_total)
    target_sq = jnp.sum(jnp.square(target_feats.astype(jnp.float32)), axis=1)
    gathered = lax.all_gather(source_feats, "tgt", axis=0, tiled=True)
    cross = lax.dot_general(
        gathered, target_feats, (((1,), (1,)), ((), ())), preferred_element_type=jnp.float32
    )
    gathered_sq = jnp.sum(jnp.square(gathered.astype(jnp.float32)), axis=1)
    cost = (gathered_sq[:, None] + target_sq[None, :] - 2.0 * cross) * scale
    potential_tgt = jnp.zeros((target_feats.shape[0],), jnp.float32)
    potential_src = jnp.zeros((source_count,), jnp.float32)
    for step in range(ITERS):
        scores = (log_target + potential_tgt)[None, :] - cost
        top = lax.pmax(jnp.max(scores, axis=1), "tgt")
        total = lax.psum(jnp.sum(jnp.exp(scores - top[:, None]), axis=1), "tgt")
        potential_src = -(top + jnp.log(total))
        column = (log_source + potential_src)[:, None] - cost
        column_top = jnp.max(column, axis=0)
        potential_tgt = -(
            column_top + jnp.log(jnp.sum(jnp.exp(column - column_top[None, :]), axis=0))
        )
    plan = jnp.exp(
        math.log(source_count)
        + (log_source + potential_src)[:, None]
        + (log_target + potential_tgt)[None, :]
        - cost
    ).astype(jnp.bfloat16)
    row_mass = jnp.sum(plan.astype(jnp.float32), axis=1)
    row_part = jnp.dot(plan, target_feats, preferred_element_type=jnp.float32)
    share_part, share_mass = (
        lax.psum_scatter(row_part, "tgt", scatter_dimension=0, tiled=True),
        lax.psum_scatter(row_mass, "tgt", scatter_dimension=0, tiled=True),
    )
    grad_source = share_mass[:, None] * source_feats.astype(jnp.float32) - share_part
    col_part = lax.dot_general(
        plan, gathered, (((0,), (0,)), ((), ())), preferred_element_type=jnp.float32
    )
    col_mass = jnp.sum(plan.astype(jnp.float32), axis=0)
    grad_target = (
        target_count
        / source_count
        * (col_mass[:, None] * target_feats.astype(jnp.float32) - col_part)
    )
    return (grad_source, grad_target, potential_src, potential_tgt)


def solution(mesh):
    return jax.shard_map(
        per_device,
        mesh=mesh,
        in_specs=(
            P(("groups", "tgt"), None),
            P(("groups", "tgt"), None),
            P("groups"),
            P(("groups", "tgt")),
        ),
        out_specs=(
            P(("groups", "tgt"), None),
            P(("groups", "tgt"), None),
            P("groups"),
            P(("groups", "tgt")),
        ),
        check_vma=False,
    )
```

profile of v0, /device:TPU:0, one launch (start us, length us, event | category | flops | bytes accessed | tf_op | source)
XLA Modules:
  0.0 395.1 jit_solution(12551948818565337685)
XLA Ops:
  7.2 0.0 copy-start.5
  7.2 0.0 all-gather.2.cloned.1.call-start
  7.2 0.7 all-gather.2.cloned.1.call-update
  7.9 0.0 reduce-scatter.2.cloned.1.call-start
  8.0 1.3 exponential_reduce_fusion.7
  9.3 36.0 %psum.28 = f32[]{:T(128)} all-reduce(f32[]{:T(128)} %exponential_reduce_fusion.7), channel_id=1, replica_groups=mesh['groups'=2,'tgt'=16] {'tgt'}, use_global_device_ids=true, to_apply=%region_2.0 | all-reduce | flops 1 | bytes 8 | tf_op jit(solution)/shard_map/psum | solution.py:16
  45.9 1.3 exponential_reduce_fusion.6
  47.9 1.5 fusion
  49.5 0.7 broadcast_subtract_fusion
  50.2 13.4 %all-gather.2.cloned.1.call-done = bf16[2048,1024]{1,0:T(8,128)(2,1)} async-done(((bf16[128,1024]{1,0:T(8,128)(2,1)}), bf16[2048,1024]{1,0:T(8,128)(2,1)}) %all-gather.2.cloned.1.call-update) | async-done | bytes 4194320 | tf_op jit(solution)/shard_map/all_gather | solution.py:19
  63.6 3.2 multiply_reduce_fusion
  66.8 0.2 copy-done.3
  67.0 4.8 %subtract_reduce_fusion.5 = (f32[2048]{0:T(1024)S(1)}, f32[2048,512]{1,0:T(8,128)}) fusion(f32[512]{0:T(512)S(1)} %broadcast_subtract_fusion, bf16[2048,1024]{1,0:T(8,128)(2,1)S(1)} %copy-done.3, bf16[512,1024]{1,0:T(8,128)(2,1)S(1)} %copy-done.5, f32[512]{0:T(512)S(1)} %fusion, f32[2048]{0:T(1024)S(1)} %multiply_reduce_fusion), kind=kOutput, calls=%fused_computation.16 | convolution fusion | flops 2153773056 | bytes 9457664 | tf_op jit(solution)/shard_map/dot_general | solution.py:20
  71.8 31.6 %pmax.21 = f32[2048]{0:T(1024)S(1)} all-reduce(f32[2048]{0:T(1024)S(1)} %get-tuple-element.12), channel_id=1, replica_groups=mesh['groups'=2,'tgt'=16] {'tgt'}, use_global_device_ids=true, to_apply=%region_6.0 | all-reduce | flops 2048 | bytes 16384 | tf_op jit(solution)/shard_map/pmax | solution.py:29
  103.5 3.2 exponential_reduce_fusion.5
  106.7 30.0 %psum.29 = f32[2048]{0:T(1024)S(1)} all-reduce(f32[2048]{0:T(1024)S(1)} %exponential_reduce_fusion.5), channel_id=1, replica_groups=mesh['groups'=2,'tgt'=16] {'tgt'}, use_global_device_ids=true, to_apply=%region_8.0 | all-reduce | flops 2048 | bytes 16384 | tf_op jit(solution)/shard_map/psum | solution.py:30
  136.7 0.0 copy-done.6
  136.7 0.0 copy-start
  136.7 0.0 copy-start.7
  136.8 2.7 subtract_reduce_fusion.4
  139.4 0.7 copy-done
  140.2 0.8 exponential_reduce_fusion.4
  141.0 0.4 subtract_reduce_fusion.3
  141.3 30.0 %pmax.22 = f32[2048]{0:T(1024)S(1)} all-reduce(f32[2048]{0:T(1024)S(1)} %subtract_reduce_fusion.3), channel_id=1, replica_groups=mesh['groups'=2,'tgt'=16] {'tgt'}, use_global_device_ids=true, to_apply=%region_12.0 | all-reduce | flops 2048 | bytes 16384 | tf_op jit(solution)/shard_map/pmax | solution.py:29
  171.3 3.2 exponential_reduce_fusion.3
  174.5 30.0 %psum.30 = f32[2048]{0:T(1024)S(1)} all-reduce(f32[2048]{0:T(1024)S(1)} %exponential_reduce_fusion.3), channel_id=1, replica_groups=mesh['groups'=2,'tgt'=16] {'tgt'}, use_global_device_ids=true, to_apply=%region_14.0 | all-reduce | flops 2048 | bytes 16384 | tf_op jit(solution)/shard_map/psum | solution.py:30
  204.5 0.0 copy-start.1
  204.6 2.7 subtract_reduce_fusion.2
  207.3 0.7 copy-done.1
  208.0 0.8 exponential_reduce_fusion.2
  208.8 0.4 subtract_reduce_fusion.1
  209.1 30.0 %pmax.23 = f32[2048]{0:T(1024)S(1)} all-reduce(f32[2048]{0:T(1024)S(1)} %subtract_reduce_fusion.1), channel_id=1, replica_groups=mesh['groups'=2,'tgt'=16] {'tgt'}, use_global_device_ids=true, to_apply=%region_18.0 | all-reduce | flops 2048 | bytes 16384 | tf_op jit(solution)/shard_map/pmax | solution.py:29
  239.1 3.2 exponential_reduce_fusion.1
  242.3 30.2 %psum.31 = f32[2048]{0:T(1024)S(1)} all-reduce(f32[2048]{0:T(1024)S(1)} %exponential_reduce_fusion.1), channel_id=1, replica_groups=mesh['groups'=2,'tgt'=16] {'tgt'}, use_global_device_ids=true, to_apply=%region_20.0 | all-reduce | flops 2048 | bytes 16384 | tf_op jit(solution)/shard_map/psum | solution.py:30
  272.5 0.6 broadcast_add_fusion
  273.1 2.9 subtract_reduce_fusion
  276.0 0.8 exponential_reduce_fusion
  276.8 0.6 fusion.3
  277.4 1.3 convert_reduce_fusion
  278.7 5.6 %fusion.4 = f32[2048,1024]{1,0:T(8,128)} fusion(bf16[2048,512]{1,0:T(8,128)(2,1)S(1)} %get-tuple-element.6, bf16[512,1024]{1,0:T(8,128)(2,1)S(1)} %copy-done.5), kind=kOutput, calls=%fused_computation.35 | convolution fusion | flops 2147483648 | bytes 11534336 | tf_op jit(solution)/shard_map/dot_general | solution.py:44
  284.3 0.0 reduce-scatter.2.cloned.1.call-update
  284.3 0.6 copy-done.8
  284.9 0.6 dynamic-slice
  286.2 30.1 %all-reduce = f32[2048]{0:T(1024)S(1)} all-reduce(f32[2048]{0:T(1024)S(1)} %get-tuple-element.5), channel_id=2, replica_groups=mesh['groups'=2,'tgt'=16] {'tgt'}, use_global_device_ids=true, to_apply=%region_24.0.clone | all-reduce | flops 2048 | bytes 16384
  316.3 0.1 dynamic-slice.1
  316.3 5.9 %fusion.2 = f32[512,1024]{1,0:T(8,128)} fusion(bf16[512,1024]{1,0:T(8,128)(2,1)S(1)} %copy-done.5, bf16[2048,512]{1,0:T(8,128)(2,1)S(1)} %get-tuple-element.6, bf16[2048,1024]{1,0:T(8,128)(2,1)} %all-gather.2.cloned.1.call-done, f32[512]{0:T(512)S(1)} %get-tuple-element.4), kind=kOutput, calls=%fused_computation.21 | convolution fusion | flops 2149580800 | bytes 9439232 | tf_op jit(solution)/shard_map/dot_general | solution.py:50
  322.2 64.0 %reduce-scatter.2.cloned.1.call-done = f32[128,1024]{1,0:T(8,128)} async-done(((f32[2048,1024]{1,0:T(8,128)}), f32[128,1024]{1,0:T(8,128)}) %reduce-scatter.2.cloned.1.call-update) | async-done | bytes 524304 | tf_op jit(solution)/shard_map/reduce_scatter | solution.py:46
  386.3 2.0 multiply_subtract_fusion
  (13 shorter events, 0.1 us)
Async XLA Ops:
  7.2 59.6 %copy-start.5 = (bf16[512,1024]{1,0:T(8,128)(2,1)S(1)}, bf16[512,1024]{1,0:T(8,128)(2,1)}, u32[]{:S(2)}) copy-start(bf16[512,1024]{1,0:T(8,128)(2,1)} %param.5) | copy-start | bytes 3145732
  7.2 56.4 %all-gather.2.cloned.1.call-start = ((), (), s32[]{:S(2)}) async-start(), calls=%async_computation.1 | async-start | bytes 4456448 | tf_op jit(solution)/shard_map/all_gather | solution.py:19
  7.9 378.4 %reduce-scatter.2.cloned.1.call-start = ((), (), s32[]{:S(2)}) async-start(), calls=%async_computation.2 | async-start | bytes 8912896 | tf_op jit(solution)/shard_map/reduce_scatter | solution.py:46
  63.6 3.4 copy-start.3
  71.8 64.9 %copy-start.6 = (f32[2048]{0:T(1024)S(1)}, f32[2048]{0:T(1024)}, u32[]{:S(2)}) copy-start(f32[2048]{0:T(1024)} %param.6) | copy-start | bytes 24580
  136.7 3.5 copy-start
  136.7 4.2 %copy-start.7 = (f32[512]{0:T(512)S(1)}, f32[512]{0:T(512)}, u32[]{:S(2)}) copy-start(f32[512]{0:T(512)} %param.7) | copy-start | bytes 6148
  204.5 3.5 copy-start.1
  272.5 3.5 copy-start.2
  284.3 0.7 copy-start.8
  316.3 69.9 %copy-start.4 = (bf16[128,1024]{1,0:T(8,128)(2,1)S(1)}, bf16[128,1024]{1,0:T(8,128)(2,1)}, u32[]{:S(2)}) copy-start(bf16[128,1024]{1,0:T(8,128)(2,1)} %param.4) | copy-start | bytes 786436
Sparse Core Ops, SparseCore 0:
  10.2 53.3 all-gather.1
  284.4 101.8 reduce-scatter.1
where the time goes:
time: 396 us; the launch traced here: 395 us
  blocking collectives  248 us (63%)
  waiting for transfers between devices  78.1 us (20%)
  other arithmetic  33.4 us (8%)
  matrix products  16.3 us (4%)
  between operations  16.3 us (4%)
    pmax x3, blocking collectives, per_device(): top = lax.pmax(jnp.max(scores, axis=1), 'tgt')  91.6 us
    psum x3, blocking collectives, per_device(): total = lax.psum(jnp.sum(jnp.exp(scores - top[:, None]), axis=1), 'tgt')  90.2 us
    reduce_scatter x1, waiting for transfers between devices, per_device(): lax.psum_scatter(row_part, 'tgt', scatter_dimension=0, tiled=True)  64 us
    psum x1, blocking collectives, per_device(): target_total = lax.psum(jnp.sum(jnp.exp(target_logits)), 'tgt')  36 us
    unnamed x1, blocking collectives  30.1 us
    all_gather x1, waiting for transfers between devices, per_device(): gathered = lax.all_gather(source_feats, 'tgt', axis=0, tiled=True)  13.4 us
    reduce_sum x3, other arithmetic, per_device(): total = lax.psum(jnp.sum(jnp.exp(scores - top[:, None]), axis=1), 'tgt')  9.62 us
    reduce_max x3, other arithmetic, per_device(): column_top = jnp.max(column, axis=0)  8.23 us
  transfers between devices with their start and end apart: 2, of which 2 were waited for; matrix products, arithmetic and copies ran while one was open for 3% of the time, Pallas kernels for 0%

commit v1 on v0

--- a/solution.py
+++ b/solution.py
@@ -5,6 +5,13 @@
 from jax.sharding import PartitionSpec as P
 
 ITERS = 3
+
+
+def draw_the_heads(chunk, on_dim):
+    main = list(chunk.shape[1:])
+    main[on_dim] *= chunk.shape[0]
+    n_now = jnp.moveaxis(chunk, 0, on_dim).reshape(main)
+    return n_now
 
 
 def per_device(source_feats, target_feats, source_logits, target_logits):
@@ -16,7 +23,25 @@
     target_total = lax.psum(jnp.sum(jnp.exp(target_logits)), "tgt")
     log_target = target_logits - jnp.log(target_total)
     target_sq = jnp.sum(jnp.square(target_feats.astype(jnp.float32)), axis=1)
-    gathered = lax.all_gather(source_feats, "tgt", axis=0, tiled=True)
+    n_parts = lax.axis_size("tgt")
+    series = [(ii, (ii + 1) % n_parts) for ii in range(n_parts)]
+    cards = [(m, q) for q, m in series]
+    mixed_arr, inter = ([], [])
+    num = 0
+    while num < n_parts - 1:
+        if num % 2 == 0:
+            arr_now = lax.ppermute(mixed_arr[-1] if mixed_arr else source_feats, "tgt", series)
+            mixed_arr.append(arr_now)
+        else:
+            local_part = lax.ppermute(inter[-1] if inter else source_feats, "tgt", cards)
+            inter.append(local_part)
+        num += 1
+    y = jnp.stack([*mixed_arr[::-1], source_feats, *inter], axis=0)
+    now = lax.axis_index("tgt")
+    view_out = len(mixed_arr)
+    piece_now = now - view_out
+    y = y[(jnp.arange(n_parts) - piece_now) % n_parts]
+    gathered = draw_the_heads(y, 0)
     cross = lax.dot_general(
         gathered, target_feats, (((1,), (1,)), ((), ())), preferred_element_type=jnp.float32
     )

time: 396 us -> 455 us (1.15)
  starting transfers between devices: 0.08 us -> 28.2 us
  local copies, waits for them, and re-layouts: 2.98 us -> 21.6 us
  waiting for transfers between devices: 78.1 us -> 93.6 us
    ppermute x0 -> x15, waiting for transfers between devices: none -> 29 us  [the longest x8 27.9 us: per_device(): lax.ppermute(mixed_arr[-1] if mixed_arr else source_feats, 'tgt', series)]
    ppermute x0 -> x15, starting transfers between devices: none -> 28.1 us  [the longest x7 27.6 us: per_device(): lax.ppermute(inter[-1] if inter else source_feats, 'tgt', cards)]
    all_gather x1 -> x0, waiting for transfers between devices: 13.4 us -> none  [per_device(): gathered = lax.all_gather(source_feats, 'tgt', axis=0, tiled=True)]
    unnamed x20 -> x35, local copies, waits for them, and re-layouts: 2.98 us -> 15.8 us
    gather x0 -> x1, local copies, waits for them, and re-layouts: none -> 5.06 us  [per_device(): y = y[(jnp.arange(n_parts) - piece_now) % n_parts]]
  transfers between devices with their start and end apart: 2 -> 16, of which waited for: 2 -> 10; matrix products, arithmetic and copies ran while one was open for 3% -> 5% of each run, Pallas kernels for 0% -> 0%
where the time goes in v1:
time: 455 us
  blocking collectives  245 us (54%)
  waiting for transfers between devices  93.6 us (21%)
  other arithmetic  33.4 us (7%)
  starting transfers between devices  28.2 us (6%)
  local copies, waits for them, and re-layouts  21.6 us (5%)
  between operations  16.3 us (4%)
  matrix products  16.2 us (4%)
    pmax x3, blocking collectives, per_device(): top = lax.pmax(jnp.max(scores, axis=1), 'tgt')  90.5 us
    psum x3, blocking collectives, per_device(): total = lax.psum(jnp.sum(jnp.exp(scores - top[:, None]), axis=1), 'tgt')  90.2 us
    reduce_scatter x1, waiting for transfers between devices, per_device(): lax.psum_scatter(row_part, 'tgt', scatter_dimension=0, tiled=True)  64.6 us
    psum x1, blocking collectives, per_device(): target_total = lax.psum(jnp.sum(jnp.exp(target_logits)), 'tgt')  34.5 us
    unnamed x1, blocking collectives  30.1 us
    ppermute x8, waiting for transfers between devices, per_device(): lax.ppermute(mixed_arr[-1] if mixed_arr else source_feats, 'tgt', series)  27.9 us
    ppermute x7, starting transfers between devices, per_device(): lax.ppermute(inter[-1] if inter else source_feats, 'tgt', cards)  27.6 us
    unnamed x35, local copies, waits for them, and re-layouts  15.8 us
  transfers between devices with their start and end apart: 16, of which 10 were waited for; matrix products, arithmetic and copies ran while one was open for 5% of the time, Pallas kernels for 0%

profile of v1, /device:TPU:0, one launch (start us, length us, event | category | flops | bytes accessed | tf_op | source)
XLA Modules:
  0.0 454.6 jit_solution(8366816049143162161)
XLA Ops:
  7.7 9.3 %collective-permute-done = bf16[128,1024]{1,0:T(8,128)(2,1)S(1)} collective-permute-done((bf16[128,1024]{1,0:T(8,128)(2,1)}, bf16[128,1024]{1,0:T(8,128)(2,1)S(1)}, u32[]{:S(2)}, u32[]{:S(2)}) %collective-permute-start) | collective-permute-done | bytes 262176 | tf_op jit(solution)/shard_map/ppermute | solution.py:33
  17.0 4.4 collective-permute-start.8
  21.4 4.1 collective-permute-done.1
  25.6 4.6 %collective-permute-start.9 = (bf16[128,1024]{1,0:T(8,128)(2,1)S(1)}, bf16[128,1024]{1,0:T(8,128)(2,1)S(1)}, u32[]{:S(2)}, u32[]{:S(2)}) collective-permute-start(bf16[128,1024]{1,0:T(8,128)(2,1)S(1)} %collective-permute-done.8), channel_id=1, source_target_pairs={{1,0},{2,1},{3,2},{4,3},{5,4},{6,5},{7,6},{8,7},{9,8},{10,9},{11,1... | collective-permute-start | bytes 786440 | tf_op jit(solution)/shard_map/ppermute | solution.py:36
  30.2 3.8 collective-permute-done.2
  34.1 4.7 %collective-permute-start.10 = (bf16[128,1024]{1,0:T(8,128)(2,1)S(1)}, bf16[128,1024]{1,0:T(8,128)(2,1)S(1)}, u32[]{:S(2)}, u32[]{:S(2)}) collective-permute-start(bf16[128,1024]{1,0:T(8,128)(2,1)S(1)} %collective-permute-done.9), channel_id=1, source_target_pairs={{1,0},{2,1},{3,2},{4,3},{5,4},{6,5},{7,6},{8,7},{9,8},{10,9},{11,1... | collective-permute-start | bytes 786440 | tf_op jit(solution)/shard_map/ppermute | solution.py:36
  38.8 3.8 collective-permute-done.3
  42.7 4.7 %collective-permute-start.11 = (bf16[128,1024]{1,0:T(8,128)(2,1)S(1)}, bf16[128,1024]{1,0:T(8,128)(2,1)S(1)}, u32[]{:S(2)}, u32[]{:S(2)}) collective-permute-start(bf16[128,1024]{1,0:T(8,128)(2,1)S(1)} %collective-permute-done.10), channel_id=1, source_target_pairs={{1,0},{2,1},{3,2},{4,3},{5,4},{6,5},{7,6},{8,7},{9,8},{10,9},{11,1... | collective-permute-start | bytes 786440 | tf_op jit(solution)/shard_map/ppermute | solution.py:36
  47.4 3.8 collective-permute-done.4
  51.3 1.3 exponential_reduce_fusion.7
  52.6 1.3 exponential_reduce_fusion.6
  53.9 4.4 collective-permute-start.12
  58.3 1.5 collective-permute-done.5
  59.9 1.5 fusion
  61.4 0.9 collective-permute-done.12
  62.2 4.7 %collective-permute-start.13 = (bf16[128,1024]{1,0:T(8,128)(2,1)S(1)}, bf16[128,1024]{1,0:T(8,128)(2,1)S(1)}, u32[]{:S(2)}, u32[]{:S(2)}) collective-permute-start(bf16[128,1024]{1,0:T(8,128)(2,1)S(1)} %collective-permute-done.12), channel_id=1, source_target_pairs={{1,0},{2,1},{3,2},{4,3},{5,4},{6,5},{7,6},{8,7},{9,8},{10,9},{11,1... | collective-permute-start | bytes 786440 | tf_op jit(solution)/shard_map/ppermute | solution.py:36
  66.9 1.6 collective-permute-done.6
  68.5 34.5 %psum.28 = f32[]{:T(128)} all-reduce(f32[]{:T(128)} %exponential_reduce_fusion.7), channel_id=1, replica_groups=mesh['groups'=2,'tgt'=16] {'tgt'}, use_global_device_ids=true, to_apply=%region_2.0 | all-reduce | flops 1 | bytes 8 | tf_op jit(solution)/shard_map/psum | solution.py:23
  105.1 1.7 bitcast_dynamic-update-slice_fusion.15
  106.8 1.7 bitcast_dynamic-update-slice_fusion.14
  109.9 0.7 bitcast_dynamic-update-slice_fusion.11
  112.8 0.7 bitcast_dynamic-update-slice_fusion.7
  115.0 0.7 bitcast_dynamic-update-slice_fusion.4
  115.7 0.7 bitcast_dynamic-update-slice_fusion.3
  118.6 5.1 %gather_fusion = bf16[16,128,1024]{2,1,0:T(8,128)(2,1)} fusion(bf16[16,128,1024]{2,1,0:T(8,128)(2,1)} %bitcast_dynamic-update-slice_fusion, s32[1024]{0:T(1024)S(1)} %pad_clamp_fusion), kind=kCustom, calls=%fused_computation | custom fusion | bytes 8388672 | tf_op jit(solution)/shard_map/gather | solution.py:43
  123.7 3.2 multiply_reduce_fusion
  127.2 4.8 %subtract_reduce_fusion.5 = (f32[2048]{0:T(1024)S(1)}, f32[2048,512]{1,0:T(8,128)}) fusion(f32[512]{0:T(512)S(1)} %broadcast_subtract_fusion, bf16[2048,1024]{1,0:T(8,128)(2,1)S(1)} %bitcast.44, bf16[512,1024]{1,0:T(8,128)(2,1)S(1)} %copy-done.5, f32[512]{0:T(512)S(1)} %fusion, f32[2048]{0:T(1024)S(1)} %bitcast.45), kind=kOutput, calls=%fused_computation.17 | convolution fusion | flops 2153773056 | bytes 9457664 | tf_op jit(solution)/shard_map/dot_general | solution.py:45
  132.0 30.5 %pmax.21 = f32[2048]{0:T(1024)S(1)} all-reduce(f32[2048]{0:T(1024)S(1)} %get-tuple-element.12), channel_id=1, replica_groups=mesh['groups'=2,'tgt'=16] {'tgt'}, use_global_device_ids=true, to_apply=%region_6.7 | all-reduce | flops 2048 | bytes 16384 | tf_op jit(solution)/shard_map/pmax | solution.py:54
  162.5 3.2 exponential_reduce_fusion.5
  165.7 30.0 %psum.29 = f32[2048]{0:T(1024)S(1)} all-reduce(f32[2048]{0:T(1024)S(1)} %exponential_reduce_fusion.5), channel_id=1, replica_groups=mesh['groups'=2,'tgt'=16] {'tgt'}, use_global_device_ids=true, to_apply=%region_8.9 | all-reduce | flops 2048 | bytes 16384 | tf_op jit(solution)/shard_map/psum | solution.py:55
  195.7 2.7 subtract_reduce_fusion.4
  199.1 0.8 exponential_reduce_fusion.4
  200.3 30.0 %pmax.22 = f32[2048]{0:T(1024)S(1)} all-reduce(f32[2048]{0:T(1024)S(1)} %subtract_reduce_fusion.3), channel_id=1, replica_groups=mesh['groups'=2,'tgt'=16] {'tgt'}, use_global_device_ids=true, to_apply=%region_12.13 | all-reduce | flops 2048 | bytes 16384 | tf_op jit(solution)/shard_map/pmax | solution.py:54
  230.3 3.2 exponential_reduce_fusion.3
  233.5 30.2 %psum.30 = f32[2048]{0:T(1024)S(1)} all-reduce(f32[2048]{0:T(1024)S(1)} %exponential_reduce_fusion.3), channel_id=1, replica_groups=mesh['groups'=2,'tgt'=16] {'tgt'}, use_global_device_ids=true, to_apply=%region_14.15 | all-reduce | flops 2048 | bytes 16384 | tf_op jit(solution)/shard_map/psum | solution.py:55
  263.7 2.7 subtract_reduce_fusion.2
  267.1 0.8 exponential_reduce_fusion.2
  268.3 30.0 %pmax.23 = f32[2048]{0:T(1024)S(1)} all-reduce(f32[2048]{0:T(1024)S(1)} %subtract_reduce_fusion.1), channel_id=1, replica_groups=mesh['groups'=2,'tgt'=16] {'tgt'}, use_global_device_ids=true, to_apply=%region_18.19 | all-reduce | flops 2048 | bytes 16384 | tf_op jit(solution)/shard_map/pmax | solution.py:54
  298.3 3.2 exponential_reduce_fusion.1
  301.5 30.0 %psum.31 = f32[2048]{0:T(1024)S(1)} all-reduce(f32[2048]{0:T(1024)S(1)} %exponential_reduce_fusion.1), channel_id=1, replica_groups=mesh['groups'=2,'tgt'=16] {'tgt'}, use_global_device_ids=true, to_apply=%region_20.21 | all-reduce | flops 2048 | bytes 16384 | tf_op jit(solution)/shard_map/psum | solution.py:55
  332.1 2.9 subtract_reduce_fusion
  335.0 0.8 exponential_reduce_fusion
  336.3 1.3 convert_reduce_fusion
  337.7 5.6 %fusion.6 = f32[2048,1024]{1,0:T(8,128)} fusion(bf16[2048,512]{1,0:T(8,128)(2,1)S(1)} %get-tuple-element.6, bf16[512,1024]{1,0:T(8,128)(2,1)S(1)} %copy-done.5), kind=kOutput, calls=%fused_computation.59 | convolution fusion | flops 2147483648 | bytes 11534336 | tf_op jit(solution)/shard_map/dot_general | solution.py:69
  345.1 30.1 %all-reduce = f32[2048]{0:T(1024)S(1)} all-reduce(f32[2048]{0:T(1024)S(1)} %get-tuple-element.5), channel_id=2, replica_groups=mesh['groups'=2,'tgt'=16] {'tgt'}, use_global_device_ids=true, to_apply=%region_24.25.clone | all-reduce | flops 2048 | bytes 16384
  375.3 5.9 %fusion.2 = f32[512,1024]{1,0:T(8,128)} fusion(bf16[512,1024]{1,0:T(8,128)(2,1)S(1)} %copy-done.5, bf16[2048,512]{1,0:T(8,128)(2,1)S(1)} %get-tuple-element.6, bf16[2048,1024]{1,0:T(8,128)(2,1)} %bitcast.43, f32[512]{0:T(512)S(1)} %get-tuple-element.4), kind=kOutput, calls=%fused_computation.22 | convolution fusion | flops 2149580800 | bytes 9439232 | tf_op jit(solution)/shard_map/dot_general | solution.py:75
  381.2 64.6 %reduce-scatter.2.cloned.1.call-done = f32[128,1024]{1,0:T(8,128)} async-done(((f32[2048,1024]{1,0:T(8,128)}), f32[128,1024]{1,0:T(8,128)}) %reduce-scatter.2.cloned.1.call-update) | async-done | bytes 524304 | tf_op jit(solution)/shard_map/reduce_scatter | solution.py:71
  445.8 2.0 multiply_subtract_fusion
  (59 shorter events, 13.7 us)
Async XLA Ops:
  7.2 105.6 %copy-start.4 = (bf16[128,1024]{1,0:T(8,128)(2,1)S(1)}, bf16[128,1024]{1,0:T(8,128)(2,1)}, u32[]{:S(2)}) copy-start(bf16[128,1024]{1,0:T(8,128)(2,1)} %param.4) | copy-start | bytes 786436
  7.2 438.6 %reduce-scatter.2.cloned.1.call-start = ((), (), s32[]{:S(2)}) async-start(), calls=%async_computation.1 | async-start | bytes 8912896 | tf_op jit(solution)/shard_map/reduce_scatter | solution.py:71
  7.2 9.8 %collective-permute-start = (bf16[128,1024]{1,0:T(8,128)(2,1)}, bf16[128,1024]{1,0:T(8,128)(2,1)S(1)}, u32[]{:S(2)}, u32[]{:S(2)}) collective-permute-start(bf16[128,1024]{1,0:T(8,128)(2,1)} %param.4), channel_id=1, source_target_pairs={{0,1},{1,2},{2,3},{3,4},{4,5},{5,6},{6,7},{7,8},{8,9},{9,10},{10,1... | collective-permute-start | bytes 786440 | tf_op jit(solution)/shard_map/ppermute | solution.py:33
  17.0 8.5 %collective-permute-start.1 = (bf16[128,1024]{1,0:T(8,128)(2,1)S(1)}, bf16[128,1024]{1,0:T(8,128)(2,1)S(1)}, u32[]{:S(2)}, u32[]{:S(2)}) collective-permute-start(bf16[128,1024]{1,0:T(8,128)(2,1)S(1)} %collective-permute-done), channel_id=1, source_target_pairs={{0,1},{1,2},{2,3},{3,4},{4,5},{5,6},{6,7},{7,8},{8,9},{9,10},{10,1... | collective-permute-start | bytes 786440 | tf_op jit(solution)/shard_map/ppermute | solution.py:33
  17.0 8.6 %collective-permute-start.8 = (bf16[128,1024]{1,0:T(8,128)(2,1)}, bf16[128,1024]{1,0:T(8,128)(2,1)S(1)}, u32[]{:S(2)}, u32[]{:S(2)}) collective-permute-start(bf16[128,1024]{1,0:T(8,128)(2,1)} %param.4), channel_id=1, source_target_pairs={{1,0},{2,1},{3,2},{4,3},{5,4},{6,5},{7,6},{8,7},{9,8},{10,9},{11,1... | collective-permute-start | bytes 786440 | tf_op jit(solution)/shard_map/ppermute | solution.py:36
  25.5 8.6 %collective-permute-start.2 = (bf16[128,1024]{1,0:T(8,128)(2,1)S(1)}, bf16[128,1024]{1,0:T(8,128)(2,1)S(1)}, u32[]{:S(2)}, u32[]{:S(2)}) collective-permute-start(bf16[128,1024]{1,0:T(8,128)(2,1)S(1)} %collective-permute-done.1), channel_id=1, source_target_pairs={{0,1},{1,2},{2,3},{3,4},{4,5},{5,6},{6,7},{7,8},{8,9},{9,10},{10,1... | collective-permute-start | bytes 786440 | tf_op jit(solution)/shard_map/ppermute | solution.py:33
  25.6 8.5 %collective-permute-start.9 = (bf16[128,1024]{1,0:T(8,128)(2,1)S(1)}, bf16[128,1024]{1,0:T(8,128)(2,1)S(1)}, u32[]{:S(2)}, u32[]{:S(2)}) collective-permute-start(bf16[128,1024]{1,0:T(8,128)(2,1)S(1)} %collective-permute-done.8), channel_id=1, source_target_pairs={{1,0},{2,1},{3,2},{4,3},{5,4},{6,5},{7,6},{8,7},{9,8},{10,9},{11,1... | collective-permute-start | bytes 786440 | tf_op jit(solution)/shard_map/ppermute | solution.py:36
  34.1 8.6 %collective-permute-start.3 = (bf16[128,1024]{1,0:T(8,128)(2,1)S(1)}, bf16[128,1024]{1,0:T(8,128)(2,1)S(1)}, u32[]{:S(2)}, u32[]{:S(2)}) collective-permute-start(bf16[128,1024]{1,0:T(8,128)(2,1)S(1)} %collective-permute-done.2), channel_id=1, source_target_pairs={{0,1},{1,2},{2,3},{3,4},{4,5},{5,6},{6,7},{7,8},{8,9},{9,10},{10,1... | collective-permute-start | bytes 786440 | tf_op jit(solution)/shard_map/ppermute | solution.py:33
  34.1 8.6 %collective-permute-start.10 = (bf16[128,1024]{1,0:T(8,128)(2,1)S(1)}, bf16[128,1024]{1,0:T(8,128)(2,1)S(1)}, u32[]{:S(2)}, u32[]{:S(2)}) collective-permute-start(bf16[128,1024]{1,0:T(8,128)(2,1)S(1)} %collective-permute-done.9), channel_id=1, source_target_pairs={{1,0},{2,1},{3,2},{4,3},{5,4},{6,5},{7,6},{8,7},{9,8},{10,9},{11,1... | collective-permute-start | bytes 786440 | tf_op jit(solution)/shard_map/ppermute | solution.py:36
  42.7 8.6 %collective-permute-start.4 = (bf16[128,1024]{1,0:T(8,128)(2,1)S(1)}, bf16[128,1024]{1,0:T(8,128)(2,1)S(1)}, u32[]{:S(2)}, u32[]{:S(2)}) collective-permute-start(bf16[128,1024]{1,0:T(8,128)(2,1)S(1)} %collective-permute-done.3), channel_id=1, source_target_pairs={{0,1},{1,2},{2,3},{3,4},{4,5},{5,6},{6,7},{7,8},{8,9},{9,10},{10,1... | collective-permute-start | bytes 786440 | tf_op jit(solution)/shard_map/ppermute | solution.py:33
  42.7 11.2 %collective-permute-start.11 = (bf16[128,1024]{1,0:T(8,128)(2,1)S(1)}, bf16[128,1024]{1,0:T(8,128)(2,1)S(1)}, u32[]{:S(2)}, u32[]{:S(2)}) collective-permute-start(bf16[128,1024]{1,0:T(8,128)(2,1)S(1)} %collective-permute-done.10), channel_id=1, source_target_pairs={{1,0},{2,1},{3,2},{4,3},{5,4},{6,5},{7,6},{8,7},{9,8},{10,9},{11,1... | collective-permute-start | bytes 786440 | tf_op jit(solution)/shard_map/ppermute | solution.py:36
  51.3 8.6 %collective-permute-start.5 = (bf16[128,1024]{1,0:T(8,128)(2,1)S(1)}, bf16[128,1024]{1,0:T(8,128)(2,1)S(1)}, u32[]{:S(2)}, u32[]{:S(2)}) collective-permute-start(bf16[128,1024]{1,0:T(8,128)(2,1)S(1)} %collective-permute-done.4), channel_id=1, source_target_pairs={{0,1},{1,2},{2,3},{3,4},{4,5},{5,6},{6,7},{7,8},{8,9},{9,10},{10,1... | collective-permute-start | bytes 786440 | tf_op jit(solution)/shard_map/ppermute | solution.py:33
  53.9 8.3 %collective-permute-start.12 = (bf16[128,1024]{1,0:T(8,128)(2,1)S(1)}, bf16[128,1024]{1,0:T(8,128)(2,1)S(1)}, u32[]{:S(2)}, u32[]{:S(2)}) collective-permute-start(bf16[128,1024]{1,0:T(8,128)(2,1)S(1)} %collective-permute-done.11), channel_id=1, source_target_pairs={{1,0},{2,1},{3,2},{4,3},{5,4},{6,5},{7,6},{8,7},{9,8},{10,9},{11,1... | collective-permute-start | bytes 786440 | tf_op jit(solution)/shard_map/ppermute | solution.py:36
  59.8 8.6 %collective-permute-start.6 = (bf16[128,1024]{1,0:T(8,128)(2,1)S(1)}, bf16[128,1024]{1,0:T(8,128)(2,1)}, u32[]{:S(2)}, u32[]{:S(2)}) collective-permute-start(bf16[128,1024]{1,0:T(8,128)(2,1)S(1)} %collective-permute-done.5), channel_id=1, source_target_pairs={{0,1},{1,2},{2,3},{3,4},{4,5},{5,6},{6,7},{7,8},{8,9},{9,10},{10,1... | collective-permute-start | bytes 786440 | tf_op jit(solution)/shard_map/ppermute | solution.py:33
  62.2 42.9 %collective-permute-start.13 = (bf16[128,1024]{1,0:T(8,128)(2,1)S(1)}, bf16[128,1024]{1,0:T(8,128)(2,1)S(1)}, u32[]{:S(2)}, u32[]{:S(2)}) collective-permute-start(bf16[128,1024]{1,0:T(8,128)(2,1)S(1)} %collective-permute-done.12), channel_id=1, source_target_pairs={{1,0},{2,1},{3,2},{4,3},{5,4},{6,5},{7,6},{8,7},{9,8},{10,9},{11,1... | collective-permute-start | bytes 786440 | tf_op jit(solution)/shard_map/ppermute | solution.py:36
  68.5 36.6 %collective-permute-start.7 = (bf16[128,1024]{1,0:T(8,128)(2,1)}, bf16[128,1024]{1,0:T(8,128)(2,1)}, u32[]{:S(2)}, u32[]{:S(2)}) collective-permute-start(bf16[128,1024]{1,0:T(8,128)(2,1)} %collective-permute-done.6), channel_id=1, source_target_pairs={{0,1},{1,2},{2,3},{3,4},{4,5},{5,6},{6,7},{7,8},{8,9},{9,10},{10,1... | collective-permute-start | bytes 786440 | tf_op jit(solution)/shard_map/ppermute | solution.py:33
  105.1 12.8 %collective-permute-start.14 = (bf16[128,1024]{1,0:T(8,128)(2,1)S(1)}, bf16[128,1024]{1,0:T(8,128)(2,1)S(1)}, u32[]{:S(2)}, u32[]{:S(2)}) collective-permute-start(bf16[128,1024]{1,0:T(8,128)(2,1)S(1)} %collective-permute-done.13), channel_id=1, source_target_pairs={{1,0},{2,1},{3,2},{4,3},{5,4},{6,5},{7,6},{8,7},{9,8},{10,9},{11,1... | collective-permute-start | bytes 786440 | tf_op jit(solution)/shard_map/ppermute | solution.py:36
  118.6 8.3 %copy-start.5 = (bf16[512,1024]{1,0:T(8,128)(2,1)S(1)}, bf16[512,1024]{1,0:T(8,128)(2,1)}, u32[]{:S(2)}) copy-start(bf16[512,1024]{1,0:T(8,128)(2,1)} %param.5) | copy-start | bytes 3145732
  123.7 3.4 copy-start.3
  132.0 63.7 %copy-start.6 = (f32[2048]{0:T(1024)S(1)}, f32[2048]{0:T(1024)}, u32[]{:S(2)}) copy-start(f32[2048]{0:T(1024)} %param.6) | copy-start | bytes 24580
  195.7 3.5 copy-start
  195.7 4.2 copy-start.7
  263.7 3.5 copy-start.1
  331.5 3.5 copy-start.2
  343.2 0.7 copy-start.8
Sparse Core Ops, SparseCore 0:
  343.4 102.3 reduce-scatter.1
